TPU v7x, 32 devices: a whole 2x2x4 slice. The times are simulated.
32 devices in a mesh: grp: 4 (over y, x), line: 8 (over z, core).
Axes of the slice: x: 2, y: 2, z: 4, core: 2. Of those that a mesh axis runs over, the one named last changes fastest.
Arguments:
- velocity: bfloat16 [3, 1536, 96, 512], P(None, 'line', 'grp'), may hold values from -6 to 6
- vorticity: bfloat16 [3, 1536, 96, 512], P(None, 'line', 'grp'), may hold values from -6 to 6
- wall_velocity: float32 [2, 256, 96, 1536], P(None, ('grp', 'line')), may hold values from -6 to 6
- wall_vorticity: float32 [2, 256, 96, 1536], P(None, ('grp', 'line')), may hold values from -6 to 6
- keep_mask: int32 [256, 96], P(('grp', 'line')), may hold values from 0 to 1, as said below
- derivative_band: float32 [7, 1536], replicated, may hold values from -3 to 3
- eigenvalues: float32 [1536], replicated, may hold values from 0.25 to 4
- eigenbasis: float32 [1536, 1536], replicated, may hold values from -0.15625 to 0.15625
Outputs:
- new_velocity: float32 [2, 256, 96, 1536], P(None, ('grp', 'line'))
- new_vorticity: float32 [2, 256, 96, 1536], P(None, ('grp', 'line'))
Inputs may be any that keep to these rules, and one draw needn't show every extreme that they name: keep_mask is 0 wherever kx >= 170, or 32 <= kz < 64.
All inputs are finite; a program needn't handle non-finite values.
Results may differ from a plain program's by a relative error of at most 0.0003.
Values sent between devices are 32-bit elements; how exact they have to be, the bound alone decides.
A program may use at most 384 MiB of HBM per device.

v0:
```python
import math

import jax
import jax.numpy as jnp
from jax import lax
from jax.sharding import PartitionSpec as P

HIGHEST_PRECISION = lax.Precision.HIGHEST


def phase_table(indices, points):
    index_cols = jnp.arange(points, dtype=jnp.int32)[None, :]
    phase_angle = (indices[:, None] * index_cols % points).astype(jnp.float32) * (
        2.0 * math.pi / points
    )
    norm_scale = 1.0 / math.sqrt(points)
    return (jnp.cos(phase_angle) * norm_scale, jnp.sin(phase_angle) * norm_scale)


def signed_wave(indices, points):
    signed_index = jnp.where(indices < points // 2, indices, indices - points)
    return signed_index.astype(jnp.float32) / (points / 2.0)


def curl_terms(spectra, stream_wave, span_wave):
    slope_source = jnp.stack(
        [
            -stream_wave * spectra[0, 1] - span_wave * spectra[2, 1],
            stream_wave * spectra[0, 0] + span_wave * spectra[2, 0],
        ]
    )
    normal_term = jnp.stack(
        [
            -span_wave * spectra[0, 1] + stream_wave * spectra[2, 1],
            span_wave * spectra[0, 0] - stream_wave * spectra[2, 0],
        ]
    )
    return (slope_source, normal_term)


def banded(padded, band_rows, extent):
    summed = band_rows[0] * padded[..., 0:extent]
    for offset in range(1, 7):
        summed = summed + band_rows[offset] * padded[..., offset : offset + extent]
    return summed


def local(
    velocity,
    vorticity,
    wall_velocity,
    wall_vorticity,
    keep_mask,
    derivative_band,
    eigenvalues,
    eigenbasis,
):
    group_count = lax.axis_size("grp")
    line_count = lax.axis_size("line")
    group_index = lax.axis_index("grp")
    line_index = lax.axis_index("line")
    moving = velocity.astype(jnp.float32)
    turning = vorticity.astype(jnp.float32)
    lamb_vector = jnp.stack(
        [
            moving[1] * turning[2] - moving[2] * turning[1],
            moving[2] * turning[0] - moving[0] * turning[2],
            moving[0] * turning[1] - moving[1] * turning[0],
        ]
    )
    slab_depth = lamb_vector.shape[1]
    span_share = lamb_vector.shape[2]
    stream_points = lamb_vector.shape[3]
    span_points = span_share * group_count
    stream_modes = stream_points // 2
    group_modes = stream_modes // group_count
    line_modes = group_modes // line_count
    span_keep = span_points // 3
    wall_points = wall_velocity.shape[3]
    span_list = jnp.concatenate(
        [
            jnp.arange(span_keep, dtype=jnp.int32),
            jnp.arange(span_points - span_keep, span_points, dtype=jnp.int32),
        ]
    )
    span_count = span_list.shape[0]
    stream_cosine, stream_sine = phase_table(
        jnp.arange(stream_modes, dtype=jnp.int32), stream_points
    )
    stream_table = jnp.stack(
        [
            stream_cosine.reshape(group_count, group_modes, stream_points),
            -stream_sine.reshape(group_count, group_modes, stream_points),
        ],
        1,
    )
    stream_table = stream_table.reshape(2 * stream_modes, stream_points)
    stream_spectra = jnp.einsum(
        "rx,cx->rc",
        lamb_vector.reshape(-1, stream_points),
        stream_table,
        precision=HIGHEST_PRECISION,
    )
    stream_spectra = stream_spectra.reshape(3, slab_depth, span_share, 2 * stream_modes)
    span_cosine, span_sine = phase_table(span_list, span_points)
    planes = lax.all_to_all(stream_spectra, "grp", split_axis=3, concat_axis=2, tiled=True)
    count_items = planes.shape[1]
    cosine_part = jnp.einsum("qz,fnzc->fcqn", span_cosine, planes, precision=HIGHEST_PRECISION)
    sine_part = jnp.einsum("qz,fnzc->fcqn", span_sine, planes, precision=HIGHEST_PRECISION)
    cosine_part = cosine_part.reshape(3, 2, group_modes, span_count, count_items)
    sine_part = sine_part.reshape(3, 2, group_modes, span_count, count_items)
    real_part = cosine_part[:, 0] + sine_part[:, 1]
    imag_part = cosine_part[:, 1] - sine_part[:, 0]
    local_modes = jnp.stack([real_part, imag_part], 1)
    span_wave = signed_wave(span_list, span_points)[:, None]
    device_modes = (group_index * line_count + line_index) * line_modes + jnp.arange(
        line_modes, dtype=jnp.int32
    )
    device_wave = (device_modes.astype(jnp.float32) / stream_modes)[:, None, None]
    whole_lines = lax.all_to_all(local_modes, "line", split_axis=2, concat_axis=4, tiled=True)
    wave_square = device_wave * device_wave + span_wave * span_wave
    slope_source, normal_term = curl_terms(whole_lines, device_wave, span_wave)
    padded = jnp.pad(slope_source, ((0, 0), (0, 0), (0, 0), (3, 3)))
    arrived = jnp.stack(
        [wave_square * whole_lines[1] - banded(padded, derivative_band, wall_points), normal_term]
    )
    middle = jnp.zeros((2, 2, line_modes, span_points - 2 * span_keep, wall_points), jnp.float32)
    arrived = jnp.concatenate(
        [arrived[:, :, :, :span_keep], middle, arrived[:, :, :, span_keep:]], 3
    )
    keep_weight = keep_mask.astype(jnp.float32)[:, :, None]
    right_side = jnp.stack([wall_velocity, wall_vorticity]) + keep_weight * arrived
    full_wave = signed_wave(jnp.arange(span_points, dtype=jnp.int32), span_points)[:, None]
    full_square = device_wave * device_wave + full_wave * full_wave
    eigen_coeffs = jnp.einsum(
        "fpkqy,yj->fpkqj", right_side, eigenbasis, precision=HIGHEST_PRECISION
    )
    eigen_coeffs = eigen_coeffs / (eigenvalues + full_square)
    solved = jnp.einsum("fpkqj,yj->fpkqy", eigen_coeffs, eigenbasis, precision=HIGHEST_PRECISION)
    return (solved[0], solved[1])


def solution(mesh):
    placed = (
        P(None, "line", "grp", None),
        P(None, "line", "grp", None),
        P(None, ("grp", "line"), None, None),
        P(None, ("grp", "line"), None, None),
        P(("grp", "line"), None),
        P(),
        P(),
        P(),
    )
    return jax.shard_map(
        local,
        mesh=mesh,
        in_specs=placed,
        out_specs=(P(None, ("grp", "line"), None, None), P(None, ("grp", "line"), None, None)),
        check_vma=False,
    )
```

profile of v0, /device:TPU:0, one launch (start us, length us, event | category | flops | bytes accessed | tf_op | source)
XLA Modules:
  0.0 1655.5 jit_solution(10274515562087793496)
XLA Ops:
  0.7 17.1 %convert_element_type.71 = f32[3,192,24,512]{3,2,1,0:T(8,128)} convert(bf16[3,192,24,512]{3,2,1,0:T(8,128)(2,1)} %param.8) | non-fusion elementwise | flops 7077888 | bytes 42467328 | tf_op jit(solution)/shard_map/convert_element_type | solution.py:62
  20.1 10.3 convert_element_type.72
  32.6 30.8 %multiply_subtract_fusion.2 = (f32[1,192,24,512]{3,2,1,0:T(8,128)}, f32[1,192,24,512]{3,2,1,0:T(8,128)}, f32[1,192,24,512]{3,2,1,0:T(8,128)}) fusion(f32[3,192,24,512]{3,2,1,0:T(8,128)} %convert_element_type.72, f32[3,192,24,512]{3,2,1,0:T(8,128)} %convert_element_type.71), kind=kLoop, calls=%fused_computation.37 | loop fusion | flops 21233664 | bytes 84934656 | tf_op jit(solution)/shard_map/sub | solution.py:66
  63.5 51.6 %fusion = f32[3,192,24,512]{3,2,1,0:T(8,128)} fusion(f32[512,512,1,1]{1,0,3,2:T(8,128)S(1)} %bitcast.85, f32[1,192,24,512]{3,2,1,0:T(8,128)} %get-tuple-element.14, f32[1,192,24,512]{3,2,1,0:T(8,128)} %get-tuple-element.13, f32[1,192,24,512]{3,2,1,0:T(8,128)} %get-tuple-element.12), kind=kOutput, calls=%fused_computation | convolution fusion | flops 43500699648 | bytes 57671680 | tf_op jit(solution)/shard_map/rx,cx->rc/dot_general | solution.py:98
  115.1 36.9 %copy.28 = f32[3,192,24,512]{1,2,0,3:T(8,128)} copy(f32[3,192,24,512]{3,2,1,0:T(8,128)} %fusion) | data formatting | bytes 56623104 | tf_op jit(solution)/shard_map/rx,cx->rc/dot_general | solution.py:98
  152.0 11.0 all-to-all-start
  163.1 408.4 %all-to-all-done = f32[3,192,24,512]{1,2,0,3:T(8,128)} async-done(((f32[3,192,24,512]{1,2,0,3:T(8,128)}), f32[3,192,24,512]{1,2,0,3:T(8,128)}, u32[]{:S(2)}, u32[]{:S(2)}) %all-to-all-start) | async-done | bytes 28311584 | tf_op jit(solution)/shard_map/all_to_all | solution.py:106
  571.6 34.4 %copy.29 = f32[3,192,24,4,128]{4,2,3,1,0:T(8,128)} copy(f32[3,192,24,4,128]{1,2,0,4,3:T(8,128)} %bitcast.5) | data formatting | bytes 56623104 | tf_op jit(solution)/shard_map/all_to_all | solution.py:106
  606.0 26.2 %convolution_bitcast_fusion.1 = f32[3,128,64,192]{1,2,3,0:T(8,128)} fusion(f32[3,192,96,128]{3,2,1,0:T(8,128)} %bitcast.80, s32[64]{0:T(128)S(1)} %get-tuple-element.11), kind=kOutput, calls=%fused_computation.40 | convolution fusion | flops 5435879424 | bytes 47186176 | tf_op jit(solution)/shard_map/qz,fnzc->fcqn/dot_general | solution.py:108
  632.3 26.2 %convolution_bitcast_fusion = f32[3,128,64,192]{1,2,3,0:T(8,128)} fusion(f32[3,192,96,128]{3,2,1,0:T(8,128)} %bitcast.81, s32[64]{0:T(128)S(1)} %get-tuple-element.11), kind=kOutput, calls=%fused_computation.39 | convolution fusion | flops 5435879424 | bytes 47186176 | tf_op jit(solution)/shard_map/qz,fnzc->fcqn/dot_general | solution.py:109
  658.4 25.1 %copy.30 = f32[3,128,64,192]{3,2,1,0:T(8,128)} copy(f32[3,128,64,192]{1,2,3,0:T(8,128)} %convolution_bitcast_fusion.1) | data formatting | bytes 37748736 | tf_op jit(solution)/shard_map/qz,fnzc->fcqn/transpose | solution.py:108
  683.5 25.1 %copy.31 = f32[3,128,64,192]{3,2,1,0:T(8,128)} copy(f32[3,128,64,192]{1,2,3,0:T(8,128)} %convolution_bitcast_fusion) | data formatting | bytes 37748736 | tf_op jit(solution)/shard_map/qz,fnzc->fcqn/transpose | solution.py:109
  708.6 27.5 %slice_add_fusion = (f32[3,1,64,64,192]{4,3,2,1,0:T(8,128)}, f32[3,1,64,64,192]{4,3,2,1,0:T(8,128)}) fusion(f32[3,2,64,64,192]{4,3,2,1,0:T(8,128)} %bitcast.83, f32[3,2,64,64,192]{4,3,2,1,0:T(8,128)} %bitcast.82), kind=kLoop, calls=%fused_computation.24 | loop fusion | flops 4718592 | bytes 56623104 | tf_op jit(solution)/shard_map/add | solution.py:112
  736.1 9.4 pad_maximum_fusion
  745.5 8.6 copy.32
  754.2 6.6 all-to-all-start.1
  761.2 2.6 broadcast_add_fusion
  763.7 540.4 %all-to-all-done.1 = f32[3,2,64,64,192]{4,3,1,0,2:T(8,128)} async-done(((f32[3,2,64,64,192]{4,3,1,0,2:T(8,128)}), f32[3,2,64,64,192]{4,3,1,0,2:T(8,128)}, u32[]{:S(2)}, u32[]{:S(2)}) %all-to-all-start.1) | async-done | bytes 18874400 | tf_op jit(solution)/shard_map/all_to_all | solution.py:120
  1304.1 26.5 %copy.35 = f32[3,2,8,64,8,192]{5,4,3,2,1,0:T(8,128)} copy(f32[3,2,8,64,8,192]{5,3,1,0,2,4:T(8,128)} %bitcast.20) | data formatting | bytes 37748736 | tf_op jit(solution)/shard_map/all_to_all | solution.py:120
  1330.7 25.3 %all_to_all.33 = f32[3,2,8,64,1536]{4,3,2,1,0:T(8,128)} reshape(f32[3,2,8,64,8,192]{5,4,3,2,1,0:T(8,128)} %copy.35) | data formatting | bytes 37748736 | tf_op jit(solution)/shard_map/all_to_all | solution.py:120
  1355.9 17.5 %copy.33 = f32[3,2,64,64,192]{4,3,2,1,0:T(8,128)} copy(f32[3,2,64,64,192]{4,3,1,0,2:T(8,128)} %all-to-all-done.1) | data formatting | bytes 37748736 | tf_op jit(solution)/shard_map/all_to_all | solution.py:120
  1373.5 4.0 slice.150
  1377.5 9.9 copy.34
  1387.4 9.5 squeeze.14
  1396.9 5.6 multiply_add_fusion.1
  1402.5 3.1 pad_maximum_fusion.1
  1405.6 3.1 maximum_bitcast_fusion
  1408.8 23.5 %subtract_bitcast_fusion = f32[1,2,8,64,1536]{4,3,2,1,0:T(8,128)} fusion(f32[2,8,64,1536]{3,2,1,0:T(8,128)} %pad_maximum_fusion.1, f32[2,8,64,1536]{3,2,1,0:T(8,128)} %squeeze.14, f32[1536]{0:T(1024)S(1)} %get-tuple-element.7, f32[1536]{0:T(1024)S(1)} %get-tuple-element.8, f32[1536]{0:T(1024)S(1)} %get-tuple-element.3, f32[1536]{0:T(1024)S(1)} %get-tuple-element.4, ...), kind=kLoop, calls=%fused_computation.44 | loop fusion | flops 23592960 | bytes 18919424 | tf_op jit(solution)/shard_map/stack | solution.py:124
  1432.3 6.3 fusion.28
  1438.6 105.2 %fusion.9 = f32[2,2,8,96,1536]{4,3,2,1,0:T(8,128)} fusion(f32[1,2,8,64,1536]{4,3,2,1,0:T(8,128)} %maximum_bitcast_fusion, f32[1,2,8,64,1536]{4,3,2,1,0:T(8,128)} %subtract_bitcast_fusion, f32[1,2,8,96,1536]{4,3,2,1,0:T(8,128)} %bitcast.86, f32[1,2,8,96,1536]{4,3,2,1,0:T(8,128)} %bitcast.87, f32[2,2,8,32,1536]{4,3,2,1,0:T(8,128)} %fusion.28, ...), kind=kOutput, calls=%fused_computation.11 | convolution fusion | flops 87015555072 | bytes 66063744 | tf_op jit(solution)/shard_map/fpkqy,yj->fpkqj/dot_general | solution.py:135
  1543.8 99.0 %fusion.19 = f32[2,2,8,96,1536]{4,3,2,1,0:T(8,128)} fusion(f32[2,2,8,96,1536]{4,3,2,1,0:T(8,128)} %fusion.9, f32[1536,1536]{1,0:T(8,128)} %param.15, f32[8,96,1536]{2,1,0:T(8,128)} %broadcast_add_fusion), kind=kOutput, calls=%fused_computation.21 | convolution fusion | flops 86977806336 | bytes 51904512 | tf_op jit(solution)/shard_map/fpkqj,yj->fpkqy/dot_general | solution.py:139
  1642.7 12.6 slice_bitcast_fusion
  (24 shorter events, 5.2 us)
Async XLA Ops:
  0.6 19.5 %copy-start = (bf16[3,192,24,512]{3,2,1,0:T(8,128)(2,1)S(1)}, bf16[3,192,24,512]{3,2,1,0:T(8,128)(2,1)}, u32[]{:S(2)}) copy-start(bf16[3,192,24,512]{3,2,1,0:T(8,128)(2,1)} %param.9) | copy-start | bytes 42467332
  152.0 419.6 %all-to-all-start = ((f32[3,192,24,512]{1,2,0,3:T(8,128)}), f32[3,192,24,512]{1,2,0,3:T(8,128)}, u32[]{:S(2)}, u32[]{:S(2)}) async-start(f32[3,192,24,512]{1,2,0,3:T(8,128)} %copy.28), calls=%async_computation | async-start | bytes 75497472 | tf_op jit(solution)/shard_map/all_to_all | solution.py:106
  754.2 6.6 copy-start.3
  754.2 6.7 copy-start.1
  754.2 7.0 copy-start.2
  754.2 550.0 %all-to-all-start.1 = ((f32[3,2,64,64,192]{4,3,1,0,2:T(8,128)}), f32[3,2,64,64,192]{4,3,1,0,2:T(8,128)}, u32[]{:S(2)}, u32[]{:S(2)}) async-start(f32[3,2,64,64,192]{4,3,1,0,2:T(8,128)} %copy.32), calls=%async_computation.1 | async-start | bytes 50331648 | tf_op jit(solution)/shard_map/all_to_all | solution.py:120
where the time goes:
time: 1660 us
  waiting for transfers between devices  949 us (57%)
  matrix products  308 us (19%)
  local copies, waits for them, and re-layouts  238 us (14%)
  other arithmetic  142 us (9%)
  starting transfers between devices  17.6 us (1%)
    all_to_all x1, waiting for transfers between devices, local(): lax.all_to_all(local_modes, 'line', split_axis=2, concat_axis=4, tiled=True)  540 us
    all_to_all x1, waiting for transfers between devices, local(): lax.all_to_all(stream_spectra, 'grp', split_axis=3, concat_axis=2, tiled=...  408 us
    dot_general x1, matrix products, local(): jnp.einsum('fpkqy,yj->fpkqj', right_side, eigenbasis, precision=HIGHEST_P...  105 us
    dot_general x1, matrix products, local(): jnp.einsum('fpkqj,yj->fpkqy', eigen_coeffs, eigenbasis, precision=HIGHEST...  99 us
    all_to_all x3, local copies, waits for them, and re-layouts, local(): lax.all_to_all(local_modes, 'line', split_axis=2, concat_axis=4, tiled=True)  69.3 us
    dot_general x1, matrix products, local(): jnp.einsum('rx,cx->rc', lamb_vector.reshape(-1, stream_points), stream_ta...  51.6 us
    dot_general x1, local copies, waits for them, and re-layouts, local(): jnp.einsum('rx,cx->rc', lamb_vector.reshape(-1, stream_points), stream_ta...  36.9 us
    all_to_all x1, local copies, waits for them, and re-layouts, local(): lax.all_to_all(stream_spectra, 'grp', split_axis=3, concat_axis=2, tiled=...  34.4 us
  transfers between devices with their start and end apart: 2, of which 2 were waited for; matrix products, arithmetic and copies ran while one was open for 0% of the time, Pallas kernels for 0%

commit v1 on v0

v1 whole, which is shorter than its diff:
```python
import math

import jax
import jax.numpy as jnp
from jax import lax
from jax.experimental import pallas as pl
from jax.experimental.pallas import tpu as pltpu
from jax.sharding import PartitionSpec as P


CHUNKS = 6
AHEAD = 3
REACH = 3
HIGH = lax.Precision.HIGH


def phase_table(indices, points, places=None):
    if places is None:
        places = jnp.arange(points, dtype=jnp.int32)
    index_cols = places[None, :]
    phase_angle = (indices[:, None] * index_cols % points).astype(jnp.float32) * (
        2.0 * math.pi / points
    )
    norm_scale = 1.0 / math.sqrt(points)
    return (jnp.cos(phase_angle) * norm_scale, jnp.sin(phase_angle) * norm_scale)


def signed_wave(indices, points):
    signed_index = jnp.where(indices < points // 2, indices, indices - points)
    return signed_index.astype(jnp.float32) / (points / 2.0)


def split_table(table):
    high = lax.reduce_precision(table, 8, 7)
    return high.astype(jnp.bfloat16), (table - high).astype(jnp.bfloat16)


def split_value(value):
    high = value.astype(jnp.bfloat16)
    return high, (value - high.astype(jnp.float32)).astype(jnp.bfloat16)


def mul(left, right):
    return lax.dot_general(
        left, right, (((1,), (0,)), ((), ())), preferred_element_type=jnp.float32
    )


def stream_kernel(u_ref, w_ref, high_ref, low_ref, *out_refs):
    rows, span, width = out_refs[0].shape[1:]
    u = [u_ref[f].astype(jnp.float32) for f in range(3)]
    w = [w_ref[f].astype(jnp.float32) for f in range(3)]
    high, low = high_ref[...], low_ref[...]
    for f in range(3):
        a, b = (f + 1) % 3, (f + 2) % 3
        lamb = u[a] * w[b] - u[b] * w[a]
        lamb = lamb.reshape(rows * span, lamb.shape[-1])
        lamb_high, lamb_low = split_value(lamb)
        spectra = mul(lamb_high, low) + mul(lamb_low, high) + mul(lamb_high, high)
        for g, out_ref in enumerate(out_refs):
            out_ref[f] = spectra[:, g * width : (g + 1) * width].reshape(rows, span, width)


def stream_stage(velocity, vorticity, table, groups, width, chunk):
    _, depth, span, points = velocity.shape
    rows_all = depth // CHUNKS
    rows = math.gcd(rows_all, 8)
    steps = rows_all // rows
    source = pl.BlockSpec((3, rows, span, points), lambda i: (0, chunk * steps + i, 0, 0))
    whole = pl.BlockSpec(table[0].shape, lambda i: (0, 0))
    return pl.pallas_call(
        stream_kernel,
        grid=(steps,),
        in_specs=[source, source, whole, whole],
        out_specs=[pl.BlockSpec((3, rows, span, width), lambda i: (0, i, 0, 0))] * groups,
        out_shape=[jax.ShapeDtypeStruct((3, rows_all, span, width), jnp.float32)] * groups,
        cost_estimate=pl.CostEstimate(
            flops=18 * rows_all * span * points * table[0].shape[1],
            bytes_accessed=12 * rows_all * span * (points + groups * width),
            transcendentals=0,
        ),
        compiler_params=pltpu.CompilerParams(vmem_limit_bytes=48 * 1024 * 1024),
        name="stream",
    )(velocity, vorticity, *table)


def make_span_kernel(steps, rows, lines, line_modes):
    def kernel(
        band_ref, wide_ref, low_ref, ax_ref, az_ref, sign_ref, slope_in, rest_in, *refs
    ):
        plane_refs = refs[:-5]
        out_ref, slope_out, rest_out, slope_ref, rest_ref = refs[-5:]
        step = pl.program_id(0)
        kept, width = ax_ref.shape

        @pl.when(step == 0)
        def _():
            slope_ref[0 : 2 * REACH] = slope_in[...]
            rest_ref[0:REACH] = rest_in[...]

        @pl.when(step > 0)
        def _():
            for r in range(2 * REACH):
                slope_ref[r] = slope_ref[rows + r]
            for r in range(REACH):
                rest_ref[r] = rest_ref[rows + r]

        @pl.when(step < steps)
        def _():
            ax, az, sign = ax_ref[...], az_ref[...], sign_ref[...]
            square = ax * ax + az * az

            for r in range(rows):
                plane = jnp.concatenate(
                    [
                        jnp.concatenate([plane_ref[f, r] for plane_ref in plane_refs], 0)
                        for f in range(3)
                    ],
                    1,
                )
                high, low = split_value(plane)
                both = mul(wide_ref[...], jnp.concatenate([high, low], 0)) + mul(
                    low_ref[...], high
                )
                cosine = [both[:kept, f * width : (f + 1) * width] for f in range(3)]
                sine = [both[kept:, f * width : (f + 1) * width] for f in range(3)]
                half = width // 2
                slope_ref[2 * REACH + r] = (ax * sine[0] + az * sine[2]) - sign * pltpu.roll(
                    ax * cosine[0] + az * cosine[2], half, 1
                )
                rest_ref[REACH + r, 0] = square * (cosine[1] + sign * pltpu.roll(sine[1], half, 1))
                rest_ref[REACH + r, 1] = (az * sine[0] - ax * sine[2]) - sign * pltpu.roll(
                    az * cosine[0] - ax * cosine[2], half, 1
                )

        @pl.when(step >= steps)
        def _():
            for r in range(rows):
                slope_ref[2 * REACH + r] = jnp.zeros((kept, width), jnp.float32)
                rest_ref[REACH + r] = jnp.zeros((2, kept, width), jnp.float32)

        group_modes = width // 2
        for r in range(rows):
            total = rest_ref[r, 0]
            for d in range(2 * REACH + 1):
                total = total - band_ref[d, step * rows + r] * slope_ref[r + d]
            turned = jnp.concatenate([total, rest_ref[r, 1]], 0).T
            for p in range(2):
                for line in range(lines):
                    at = p * group_modes + line * line_modes
                    out_ref[line, r, p] = turned[at : at + line_modes]

        slope_out[...] = slope_ref[rows : rows + 2 * REACH]
        rest_out[...] = rest_ref[rows : rows + REACH]

    return kernel


def span_stage(planes, band, wide, low, ax, az, sign, carry, lines, flush):
    sources = len(planes)
    _, rows_all, span, width = planes[0].shape
    kept = ax.shape[0]
    rows = math.gcd(rows_all, 8)
    steps = rows_all // rows
    extra = -(-2 * REACH // rows) if flush else 0
    line_modes = width // 2 // lines
    whole = lambda shape: pl.BlockSpec(shape, lambda i: (0,) * len(shape))
    held = [
        jax.ShapeDtypeStruct((2 * REACH, kept, width), jnp.float32),
        jax.ShapeDtypeStruct((REACH, 2, kept, width), jnp.float32),
    ]
    rows_out = (steps + extra) * rows
    return pl.pallas_call(
        make_span_kernel(steps, rows, lines, line_modes),
        grid=(steps + extra,),
        in_specs=[
            pl.BlockSpec(memory_space=pltpu.SMEM),
            whole(wide.shape),
            whole(low.shape),
            whole(ax.shape),
            whole(az.shape),
            whole(sign.shape),
            whole(held[0].shape),
            whole(held[1].shape),
        ]
        + [
            pl.BlockSpec(
                (3, rows, span, width), lambda i: (0, jnp.minimum(i, steps - 1), 0, 0)
            )
        ]
        * sources,
        out_specs=[
            pl.BlockSpec((lines, rows, 2, line_modes, 2 * kept), lambda i: (0, i, 0, 0, 0)),
            whole(held[0].shape),
            whole(held[1].shape),
        ],
        out_shape=[
            jax.ShapeDtypeStruct((lines, rows_out, 2, line_modes, 2 * kept), jnp.float32)
        ]
        + held,
        scratch_shapes=[
            pltpu.VMEM((rows + 2 * REACH, kept, width), jnp.float32),
            pltpu.VMEM((rows + REACH, 2, kept, width), jnp.float32),
        ],
        cost_estimate=pl.CostEstimate(
            flops=40 * rows_all * sources * span * width * kept,
            bytes_accessed=12 * rows_all * span * sources * width,
            transcendentals=0,
        ),
        compiler_params=pltpu.CompilerParams(vmem_limit_bytes=48 * 1024 * 1024),
        name="spanwise",
    )(band, wide, low, ax, az, sign, *carry, *planes)


def local(
    velocity,
    vorticity,
    wall_velocity,
    wall_vorticity,
    keep_mask,
    derivative_band,
    eigenvalues,
    eigenbasis,
):
    groups = lax.axis_size("grp")
    lines = lax.axis_size("line")
    group_index = lax.axis_index("grp")
    line_index = lax.axis_index("line")
    depth, span_share, stream_points = velocity.shape[1:]
    span_points = span_share * groups
    stream_modes = stream_points // 2
    group_modes = stream_modes // groups
    line_modes = group_modes // lines
    wall_points = wall_velocity.shape[3]
    width = 2 * group_modes
    span_keep = span_points // 3
    kept = 2 * span_keep
    live_groups = min(groups, -(-(2 * stream_modes // 3) // group_modes))

    partners = group_index ^ jnp.arange(groups, dtype=jnp.int32)
    partner_modes = (
        partners[:, None] * group_modes + jnp.arange(group_modes, dtype=jnp.int32)
    ).reshape(-1)
    cosine, sine = phase_table(partner_modes, stream_points)
    stream_table = jnp.stack(
        [
            cosine.reshape(groups, group_modes, stream_points),
            -sine.reshape(groups, group_modes, stream_points),
        ],
        1,
    ).reshape(2 * stream_modes, stream_points)
    stream_table = split_table(stream_table.T)

    span_list = jnp.concatenate(
        [
            jnp.arange(span_keep, dtype=jnp.int32),
            jnp.arange(span_points - span_keep, span_points, dtype=jnp.int32),
        ]
    )
    places = (
        partners[:, None] * span_share + jnp.arange(span_share, dtype=jnp.int32)
    ).reshape(-1)
    span_high, span_low = split_table(
        jnp.concatenate(phase_table(span_list, span_points, places), 0)
    )
    span_wide = jnp.concatenate([span_high, span_high], 1)
    mode_at = group_index * group_modes + jnp.arange(group_modes, dtype=jnp.int32)
    ax = mode_at.astype(jnp.float32) / stream_modes
    ax = jnp.broadcast_to(jnp.concatenate([ax, ax])[None, :], (kept, width))
    az = jnp.broadcast_to(signed_wave(span_list, span_points)[:, None], (kept, width))
    sign = jnp.where(jnp.arange(width) < group_modes, 1.0, -1.0).astype(jnp.float32)
    sign = jnp.broadcast_to(sign[None, :], (kept, width))

    pad_rows = 2 * REACH + 8
    band_padded = jnp.pad(derivative_band, ((0, 0), (pad_rows, pad_rows)))
    basis_padded = jnp.pad(eigenbasis, ((pad_rows, pad_rows), (0, 0)))

    chunk_rows = depth // CHUNKS
    carry = (
        jnp.zeros((2 * REACH, kept, width), jnp.float32),
        jnp.zeros((REACH, 2, kept, width), jnp.float32),
    )
    spectra = [
        stream_stage(velocity, vorticity, stream_table, groups, width, chunk)
        for chunk in range(CHUNKS)
    ]
    planes = []
    for own in spectra:
        blocks = [own[0]]
        for d in range(1, groups):
            pairs = [(g, g ^ d) for g in range(groups) if g ^ d < live_groups]
            blocks.append(lax.ppermute(own[d], "grp", pairs))
        planes.append(blocks)
    walls = [wall_velocity, wall_vorticity]
    wall_coeffs = []
    arrived = None
    for chunk in range(CHUNKS):
        flush = chunk == CHUNKS - 1
        rows = math.gcd(chunk_rows, 8)
        rows_out = chunk_rows + (-(-2 * REACH // rows) * rows if flush else 0)
        start = pad_rows + line_index * depth + chunk * chunk_rows - REACH
        band = lax.dynamic_slice_in_dim(band_padded, start, rows_out, 1)
        if chunk == 0:
            ahead = [planes[c][0] for c in range(1, min(AHEAD, CHUNKS - 1) + 1)]
            *ahead, band = lax.optimization_barrier((*ahead, band))
            for c, block in enumerate(ahead, 1):
                planes[c][0] = block
        elif chunk + AHEAD < CHUNKS:
            planes[chunk + AHEAD][0], band = lax.optimization_barrier(
                (planes[chunk + AHEAD][0], band)
            )
        if chunk < len(walls):
            coeffs = jnp.einsum("pkqy,yj->pkqj", walls[chunk], eigenbasis, precision=HIGH)
            coeffs, band = lax.optimization_barrier((coeffs, band))
            wall_coeffs.append(coeffs)
        out, *carry = span_stage(
            planes[chunk], band, span_wide, span_low, ax, az, sign, carry, lines, flush
        )
        whole_lines = lax.all_to_all(out, "line", split_axis=0, concat_axis=0, tiled=True)
        first = pad_rows + chunk * chunk_rows - REACH
        basis = jnp.stack(
            [
                lax.slice_in_dim(basis_padded, first + s * depth, first + s * depth + rows_out)
                for s in range(lines)
            ]
        ).reshape(lines * rows_out, wall_points)
        part = jnp.einsum(
            "yr,yj->rj",
            whole_lines.reshape(lines * rows_out, -1),
            basis,
            precision=HIGH,
        )
        arrived = part if arrived is None else arrived + part
    arrived = arrived.reshape(2, line_modes, 2, kept, wall_points)

    device_modes = (group_index * lines + line_index) * line_modes + jnp.arange(
        line_modes, dtype=jnp.int32
    )
    device_wave = (device_modes.astype(jnp.float32) / stream_modes)[:, None, None]
    full_wave = signed_wave(jnp.arange(span_points, dtype=jnp.int32), span_points)[:, None]
    full_square = device_wave * device_wave + full_wave * full_wave
    keep_weight = keep_mask.astype(jnp.float32)[:, :, None]
    solved = []
    for field, coeffs in enumerate(wall_coeffs):
        forced = arrived[:, :, field]
        middle = jnp.zeros(
            (2, line_modes, span_points - kept, wall_points), jnp.float32
        )
        forced = jnp.concatenate([forced[:, :, :span_keep], middle, forced[:, :, span_keep:]], 2)
        coeffs = (coeffs + keep_weight * forced) / (eigenvalues + full_square)
        solved.append(jnp.einsum("pkqj,yj->pkqy", coeffs, eigenbasis, precision=HIGH))
    return tuple(solved)


def solution(mesh):
    placed = (
        P(None, "line", "grp", None),
        P(None, "line", "grp", None),
        P(None, ("grp", "line"), None, None),
        P(None, ("grp", "line"), None, None),
        P(("grp", "line"), None),
        P(),
        P(),
        P(),
    )

    return jax.shard_map(
        local,
        mesh=mesh,
        in_specs=placed,
        out_specs=(P(None, ("grp", "line"), None, None), P(None, ("grp", "line"), None, None)),
        check_vma=False,
    )
```

time: 1660 us -> 689 us (0.42)
  the two profiles are of different devices: /device:TPU:0 before, /device:TPU:11 now
where the time goes in v1:
time: 689 us; the launch traced here: 682 us
  matrix products  194 us (28%)
  waiting for transfers between devices  181 us (26%)
  starting transfers between devices  83.9 us (12%)
  local copies, waits for them, and re-layouts  82.5 us (12%)
  Pallas kernels  80 us (12%)
  blocking collectives  53.7 us (8%)
    ppermute x18, waiting for transfers between devices, local(): blocks.append(lax.ppermute(own[d], 'grp', pairs))  158 us
    dot_general x6, matrix products, local(): jnp.einsum('yr,yj->rj', whole_lines.reshape(lines * rows_out, -1), basis,...  78.5 us
    dot_general x2, matrix products, local(): jnp.einsum('pkqj,yj->pkqy', coeffs, eigenbasis, precision=HIGH)  60.9 us
    dot_general x2, matrix products, local(): jnp.einsum('pkqy,yj->pkqj', walls[chunk], eigenbasis, precision=HIGH)  54.3 us
    all_to_all x1, blocking collectives, local(): lax.all_to_all(out, 'line', split_axis=0, concat_axis=0, tiled=True)  53.7 us
    ppermute x18, starting transfers between devices, local(): blocks.append(lax.ppermute(own[d], 'grp', pairs))  48.4 us
    unnamed x90, local copies, waits for them, and re-layouts  45.4 us
    pallas_call x6, Pallas kernels, stream_stage(): pl.pallas_call(stream_kernel, grid=(steps,), in_specs=[source, source, wh...  41.5 us
  transfers between devices with their start and end apart: 23, of which 8 were waited for; matrix products, arithmetic and copies ran while one was open for 22% of the time, Pallas kernels for 10%

profile of v1, /device:TPU:11, one launch (start us, length us, event | category | flops | bytes accessed | tf_op | source)
XLA Modules:
  0.0 681.8 jit_solution(10095877786751818525)
XLA Ops:
  3.5 7.5 %stream.9 = (f32[3,32,24,128]{3,2,1,0:T(8,128)S(1)}, f32[3,32,24,128]{3,2,1,0:T(8,128)}, f32[3,32,24,128]{3,2,1,0:T(8,128)}, f32[3,32,24,128]{3,2,1,0:T(8,128)}) custom-call(bf16[3,192,24,512]{3,2,1,0:T(8,128)(2,1)} %u_ref.11, bf16[3,192,24,512]{3,2,1,0:T(8,128)(2,1)} %w_ref.11, bf16[512,512]{1,0:T(8,128)(2,1)S(1)} %get-tuple-element.155.high_ref, ...), custom_call_target="tpu_custom_call" | custom-call | flops 3623878656 | bytes 9437184 | tf_op jit(solution)/shard_map/stream/pallas_call | solution.py:71
  20.7 7.3 %stream.6 = (f32[3,32,24,128]{3,2,1,0:T(8,128)S(1)}, f32[3,32,24,128]{3,2,1,0:T(8,128)}, f32[3,32,24,128]{3,2,1,0:T(8,128)}, f32[3,32,24,128]{3,2,1,0:T(8,128)S(1)}) custom-call(bf16[3,192,24,512]{3,2,1,0:T(8,128)(2,1)} %u_ref.11, bf16[3,192,24,512]{3,2,1,0:T(8,128)(2,1)} %w_ref.11, bf16[512,512]{1,0:T(8,128)(2,1)S(1)} %get-tuple-element.155.high_ref, ...), custom_call_target="tpu_custom_call" | custom-call | flops 3623878656 | bytes 9437184 | tf_op jit(solution)/shard_map/stream/pallas_call | solution.py:71
  31.4 27.0 %fusion.18 = f32[2,8,96,1536]{3,2,1,0:T(8,128)} fusion(f32[2,8,96,1536]{3,2,1,0:T(8,128)} %param.10, f32[1536,1536]{1,0:T(8,128)S(1)} %bitcast.157), kind=kOutput, calls=%fused_computation.19 | convolution fusion | flops 21743271936 | bytes 28311552 | tf_op jit(solution)/shard_map/pkqy,yj->pkqj/dot_general | solution.py:313
  58.5 27.3 %fusion.16 = f32[2,8,96,1536]{3,2,1,0:T(8,128)} fusion(f32[2,8,96,1536]{3,2,1,0:T(8,128)} %param.11, f32[1536,1536]{1,0:T(8,128)S(1)} %bitcast.157), kind=kOutput, calls=%fused_computation.17 | convolution fusion | flops 21743271936 | bytes 28311552 | tf_op jit(solution)/shard_map/pkqy,yj->pkqj/dot_general | solution.py:313
  85.8 6.4 stream.7
  96.3 6.4 stream.8
  105.9 6.8 %stream.10 = (f32[3,32,24,128]{3,2,1,0:T(8,128)S(1)}, f32[3,32,24,128]{3,2,1,0:T(8,128)S(1)}, f32[3,32,24,128]{3,2,1,0:T(8,128)S(1)}, f32[3,32,24,128]{3,2,1,0:T(8,128)S(1)}) custom-call(bf16[3,192,24,512]{3,2,1,0:T(8,128)(2,1)} %u_ref.11, bf16[3,192,24,512]{3,2,1,0:T(8,128)(2,1)} %w_ref.11, bf16[512,512]{1,0:T(8,128)(2,1)S(1)} %get-tuple-element.155.high_ref, ...), custom_call_target="tpu_custom_call" | custom-call | flops 3623878656 | bytes 9437184 | tf_op jit(solution)/shard_map/stream/pallas_call | solution.py:71
  123.2 6.9 %spanwise.6 = (f32[8,32,2,8,128]{4,3,2,1,0:T(8,128)}, f32[6,64,128]{2,1,0:T(8,128)S(1)}, f32[3,2,64,128]{3,2,1,0:T(8,128)S(1)}) custom-call(f32[7,32]{1,0:T(8,128)S(1)} %get-tuple-element.59.band_ref, bf16[128,192]{1,0:T(8,128)(2,1)S(1)} %pad_maximum_fusion.2.wide_ref, bf16[128,96]{1,0:T(8,128)(2,1)S(1)} %get-tuple-element.156.low_ref, ...), custom_call_target="tpu_custom_call" | custom-call | flops 1006632960 | bytes 4718592 | tf_op jit(solution)/shard_map/spanwise/pallas_call | solution.py:173
  130.1 15.5 %collective-permute-done.5.refs_3_ = f32[3,32,24,128]{3,2,1,0:T(8,128)} collective-permute-done((f32[3,32,24,128]{3,2,1,0:T(8,128)}, f32[3,32,24,128]{3,2,1,0:T(8,128)}, u32[]{:S(2)}, u32[]{:S(2)}) %collective-permute-start.5) | collective-permute-done | bytes 1179680 | tf_op jit(solution)/shard_map/ppermute | solution.py:292
  145.6 6.5 spanwise.7
  152.1 53.7 %all_to_all.30 = f32[8,32,2,8,128]{4,3,2,1,0:T(8,128)} all-to-all(f32[8,32,2,8,128]{4,3,2,1,0:T(8,128)} %get-tuple-element.74), channel_id=1, replica_groups=mesh['grp'=4,'line'=8] {'line'}, dimensions={0} | all-to-all | bytes 4194304 | tf_op jit(solution)/shard_map/all_to_all | solution.py:319
  205.8 7.2 %all-to-all-start = ((f32[8,32,2,8,128]{4,3,2,1,0:T(8,128)}), f32[8,32,2,8,128]{4,3,2,1,0:T(8,128)}, u32[]{:S(2)}, u32[]{:S(2)}) async-start(f32[8,32,2,8,128]{4,3,2,1,0:T(8,128)} %get-tuple-element.64), calls=%async_computation | async-start | bytes 4194304 | tf_op jit(solution)/shard_map/all_to_all | solution.py:319
  221.6 7.1 %stream.11 = (f32[3,32,24,128]{3,2,1,0:T(8,128)S(1)}, f32[3,32,24,128]{3,2,1,0:T(8,128)S(1)}, f32[3,32,24,128]{3,2,1,0:T(8,128)S(1)}, f32[3,32,24,128]{3,2,1,0:T(8,128)}) custom-call(bf16[3,192,24,512]{3,2,1,0:T(8,128)(2,1)} %u_ref.11, bf16[3,192,24,512]{3,2,1,0:T(8,128)(2,1)} %w_ref.11, bf16[512,512]{1,0:T(8,128)(2,1)S(1)} %get-tuple-element.155.high_ref, ...), custom_call_target="tpu_custom_call" | custom-call | flops 3623878656 | bytes 9437184 | tf_op jit(solution)/shard_map/stream/pallas_call | solution.py:71
  231.7 10.6 %collective-permute-done.6.refs_1_ = f32[3,32,24,128]{3,2,1,0:T(8,128)S(1)} collective-permute-done((f32[3,32,24,128]{3,2,1,0:T(8,128)}, f32[3,32,24,128]{3,2,1,0:T(8,128)S(1)}, u32[]{:S(2)}, u32[]{:S(2)}) %collective-permute-start.6) | collective-permute-done | bytes 1179680 | tf_op jit(solution)/shard_map/ppermute | solution.py:292
  242.4 28.0 %collective-permute-done.7.refs_2_ = f32[3,32,24,128]{3,2,1,0:T(8,128)S(1)} collective-permute-done((f32[3,32,24,128]{3,2,1,0:T(8,128)}, f32[3,32,24,128]{3,2,1,0:T(8,128)S(1)}, u32[]{:S(2)}, u32[]{:S(2)}) %collective-permute-start.7) | collective-permute-done | bytes 1179680 | tf_op jit(solution)/shard_map/ppermute | solution.py:292
  289.7 47.3 %collective-permute-done.10.refs_2_ = f32[3,32,24,128]{3,2,1,0:T(8,128)S(1)} collective-permute-done((f32[3,32,24,128]{3,2,1,0:T(8,128)}, f32[3,32,24,128]{3,2,1,0:T(8,128)S(1)}, u32[]{:S(2)}, u32[]{:S(2)}) %collective-permute-start.10) | collective-permute-done | bytes 1179680 | tf_op jit(solution)/shard_map/ppermute | solution.py:292
  385.1 50.0 %collective-permute-done.13.refs_2_ = f32[3,32,24,128]{3,2,1,0:T(8,128)} collective-permute-done((f32[3,32,24,128]{3,2,1,0:T(8,128)}, f32[3,32,24,128]{3,2,1,0:T(8,128)}, u32[]{:S(2)}, u32[]{:S(2)}) %collective-permute-start.13) | collective-permute-done | bytes 1179680 | tf_op jit(solution)/shard_map/ppermute | solution.py:292
  435.1 6.5 spanwise.10
  441.6 7.4 %all-to-all-start.4 = ((f32[8,32,2,8,128]{4,3,2,1,0:T(8,128)}), f32[8,32,2,8,128]{4,3,2,1,0:T(8,128)}, u32[]{:S(2)}, u32[]{:S(2)}) async-start(f32[8,32,2,8,128]{4,3,2,1,0:T(8,128)} %get-tuple-element.97), calls=%async_computation.4 | async-start | bytes 4194304 | tf_op jit(solution)/shard_map/all_to_all | solution.py:319
  465.0 7.0 %spanwise.11 = (f32[8,40,2,8,128]{4,3,2,1,0:T(8,128)}, f32[6,64,128]{2,1,0:T(8,128)}, f32[3,2,64,128]{3,2,1,0:T(8,128)}) custom-call(f32[7,40]{1,0:T(8,128)S(1)} %pad_dynamic-slice_fusion.band_ref, bf16[128,192]{1,0:T(8,128)(2,1)S(1)} %pad_maximum_fusion.2.wide_ref, bf16[128,96]{1,0:T(8,128)(2,1)S(1)} %get-tuple-element.156.low_ref, ...), custom_call_target="tpu_custom_call" | custom-call | flops 1006632960 | bytes 4718592 | tf_op jit(solution)/shard_map/spanwise/pallas_call | solution.py:173
  472.0 22.5 %all-to-all-done.4 = f32[8,32,2,8,128]{4,3,2,1,0:T(8,128)} async-done(((f32[8,32,2,8,128]{4,3,2,1,0:T(8,128)}), f32[8,32,2,8,128]{4,3,2,1,0:T(8,128)}, u32[]{:S(2)}, u32[]{:S(2)}) %all-to-all-start.4) | async-done | bytes 2097184 | tf_op jit(solution)/shard_map/all_to_all | solution.py:319
  494.5 8.3 %all-to-all-start.5 = ((f32[8,40,2,8,128]{4,3,2,1,0:T(8,128)}), f32[8,40,2,8,128]{4,3,2,1,0:T(8,128)}, u32[]{:S(2)}, u32[]{:S(2)}) async-start(f32[8,40,2,8,128]{4,3,2,1,0:T(8,128)} %get-tuple-element.104), calls=%async_computation.5 | async-start | bytes 5242880 | tf_op jit(solution)/shard_map/all_to_all | solution.py:319
  520.9 10.0 %fusion.55 = f32[2048,1536]{1,0:T(8,128)} fusion(f32[256,2048]{1,0:T(8,128)} %reshape.256, f32[256,1536]{1,0:T(8,128)} %bitcast.22), kind=kOutput, calls=%fused_computation.141 | convolution fusion | flops 4831838208 | bytes 16252928 | tf_op jit(solution)/shard_map/yr,yj->rj/dot_general | solution.py:327
  530.8 9.6 %fusion.54 = f32[2048,1536]{1,0:T(8,128)} fusion(f32[256,2048]{1,0:T(8,128)S(1)} %copy-done.25, f32[256,1536]{1,0:T(8,128)} %bitcast.12), kind=kOutput, calls=%fused_computation.140 | convolution fusion | flops 4831838208 | bytes 16252928 | tf_op jit(solution)/shard_map/yr,yj->rj/dot_general | solution.py:327
  540.4 9.6 %fusion.56 = f32[2048,1536]{1,0:T(8,128)} fusion(f32[256,2048]{1,0:T(8,128)S(1)} %copy-done.24, f32[256,1536]{1,0:T(8,128)} %bitcast.31), kind=kOutput, calls=%fused_computation.142 | convolution fusion | flops 4831838208 | bytes 16252928 | tf_op jit(solution)/shard_map/yr,yj->rj/dot_general | solution.py:327
  550.0 9.6 %fusion.57 = f32[2048,1536]{1,0:T(8,128)} fusion(f32[256,2048]{1,0:T(8,128)S(1)} %copy-done.23, f32[256,1536]{1,0:T(8,128)} %bitcast.40), kind=kOutput, calls=%fused_computation.143 | convolution fusion | flops 4831838208 | bytes 16252928 | tf_op jit(solution)/shard_map/yr,yj->rj/dot_general | solution.py:327
  559.6 9.5 %fusion.58 = f32[2048,1536]{1,0:T(8,128)} fusion(f32[256,2048]{1,0:T(8,128)S(1)} %reshape.262, f32[256,1536]{1,0:T(8,128)} %bitcast.49), kind=kOutput, calls=%fused_computation.144 | convolution fusion | flops 4831838208 | bytes 16252928 | tf_op jit(solution)/shard_map/yr,yj->rj/dot_general | solution.py:327
  571.7 30.3 %add_add_fusion = f32[2048,1536]{1,0:T(8,128)} fusion(f32[2048,1536]{1,0:T(8,128)} %fusion.58, f32[2048,1536]{1,0:T(8,128)} %fusion.57, f32[2048,1536]{1,0:T(8,128)} %fusion.56, f32[2048,1536]{1,0:T(8,128)} %fusion.54, f32[2048,1536]{1,0:T(8,128)} %fusion.55, f32[320,2048]{1,0:T(8,128)S(1)} %reshape.264, f32[320,1536]{1,0:T(8,128)} %bitcast.58), kind=kOutput, calls=%fused_computation | convolution fusion | flops 6055526400 | bytes 80084992 | tf_op jit(solution)/shard_map/yr,yj->rj/dot_general | solution.py:327
  602.0 8.8 %slice_bitcast_fusion = (f32[2,8,64,1536]{3,2,1,0:T(8,128)}, f32[2,8,64,1536]{3,2,1,0:T(8,128)S(1)}) fusion(f32[2,8,2,64,1536]{4,3,2,1,0:T(8,128)} %bitcast.160), kind=kLoop, calls=%fused_computation.23 | loop fusion | bytes 25165824 | tf_op jit(solution)/shard_map/squeeze | solution.py:345
  610.8 6.5 fusion.52
  620.4 30.6 %fusion.9 = f32[2,8,96,1536]{3,2,1,0:T(8,128)} fusion(f32[2,8,96,1536]{3,2,1,0:T(8,128)} %fusion.16, f32[2,8,32,1536]{3,2,1,0:T(8,128)} %get-tuple-element.151, f32[2,8,32,1536]{3,2,1,0:T(8,128)} %get-tuple-element.150, f32[1536,1536]{1,0:T(8,128)S(1)} %bitcast.159, f32[96]{0:T(128)S(1)} %pad.14.clone, f32[8,96,1536]{2,1,0:T(8,128)} %broadcast_add_fusion, ...), kind=kOutput, calls=%fused_computation.11 | convolution fusion | flops 21755068416 | bytes 39325056 | tf_op jit(solution)/shard_map/pkqj,yj->pkqy/dot_general | solution.py:351
  651.0 30.3 %fusion.2 = f32[2,8,96,1536]{3,2,1,0:T(8,128)} fusion(f32[2,8,96,1536]{3,2,1,0:T(8,128)} %fusion.18, f32[2,8,32,1536]{3,2,1,0:T(8,128)S(1)} %copy-done.28, f32[2,8,32,1536]{3,2,1,0:T(8,128)S(1)} %copy-done.27, f32[1536,1536]{1,0:T(8,128)S(1)} %bitcast.159, f32[96]{0:T(128)S(1)} %pad.14.clone, f32[8,96,1536]{2,1,0:T(8,128)} %broadcast_add_fusion, ...), kind=kOutput, calls=%fused_computation.4 | convolution fusion | flops 21755068416 | bytes 39325056 | tf_op jit(solution)/shard_map/pkqj,yj->pkqy/dot_general | solution.py:351
  (171 shorter events, 152.2 us)
Async XLA Ops:
  12.0 103.9 %collective-permute-start = (f32[3,32,24,128]{3,2,1,0:T(8,128)}, f32[3,32,24,128]{3,2,1,0:T(8,128)}, u32[]{:S(2)}, u32[]{:S(2)}) collective-permute-start(f32[3,32,24,128]{3,2,1,0:T(8,128)} %get-tuple-element.61), channel_id=1, source_target_pairs={{0,8},{8,0},{24,16},{1,9},{9,1},{25,17},{2,10},{10,2},{26,18},{3,1... | collective-permute-start | bytes 3538952 | tf_op jit(solution)/shard_map/ppermute | solution.py:292
  14.2 107.6 %collective-permute-start.1 = (f32[3,32,24,128]{3,2,1,0:T(8,128)}, f32[3,32,24,128]{3,2,1,0:T(8,128)}, u32[]{:S(2)}, u32[]{:S(2)}) collective-permute-start(f32[3,32,24,128]{3,2,1,0:T(8,128)} %get-tuple-element.62), channel_id=1, source_target_pairs={{0,16},{16,0},{24,8},{1,17},{17,1},{25,9},{2,18},{18,2},{26,10},{3... | collective-permute-start | bytes 3538952 | tf_op jit(solution)/shard_map/ppermute | solution.py:292
  15.4 15.9 %slice-start = ((s8[9437184]{0:T(1024)(128)(4,1)}), s8[4194304]{0:T(1024)(128)(4,1)S(1)}, s32[]{:S(2)}) async-start(s8[9437184]{0:T(1024)(128)(4,1)} %bitcast.156), calls=%async_computation.6 | async-start | bytes 8388608
  15.5 15.9 %slice-start.1 = ((s8[9437184]{0:T(1024)(128)(4,1)}), s8[4194304]{0:T(1024)(128)(4,1)S(1)}, s32[]{:S(2)}) async-start(s8[9437184]{0:T(1024)(128)(4,1)} %bitcast.156), calls=%async_computation.7 | async-start | bytes 8388608
  15.5 15.9 %slice-start.2 = ((s8[9437184]{0:T(1024)(128)(4,1)}), s8[1048576]{0:T(1024)(128)(4,1)S(1)}, s32[]{:S(2)}) async-start(s8[9437184]{0:T(1024)(128)(4,1)} %bitcast.156), calls=%async_computation.8 | async-start | bytes 2097152
  15.5 106.3 %collective-permute-start.2 = (f32[3,32,24,128]{3,2,1,0:T(8,128)}, f32[3,32,24,128]{3,2,1,0:T(8,128)}, u32[]{:S(2)}, u32[]{:S(2)}) collective-permute-start(f32[3,32,24,128]{3,2,1,0:T(8,128)} %get-tuple-element.63), channel_id=1, source_target_pairs={{8,16},{16,8},{24,0},{9,17},{17,9},{25,1},{10,18},{18,10},{26,2},{... | collective-permute-start | bytes 3538952 | tf_op jit(solution)/shard_map/ppermute | solution.py:292
  27.9 30.5 %copy-start.6 = (f32[3,32,24,128]{3,2,1,0:T(8,128)}, f32[3,32,24,128]{3,2,1,0:T(8,128)S(1)}, u32[]{:S(2)}) copy-start(f32[3,32,24,128]{3,2,1,0:T(8,128)S(1)} %get-tuple-element.70.refs_0_) | copy-start | bytes 3538948
  27.9 30.5 %copy-start.22 = (f32[3,32,24,128]{3,2,1,0:T(8,128)}, f32[3,32,24,128]{3,2,1,0:T(8,128)S(1)}, u32[]{:S(2)}) copy-start(f32[3,32,24,128]{3,2,1,0:T(8,128)S(1)} %get-tuple-element.73) | copy-start | bytes 3538948
  27.9 102.2 %collective-permute-start.3 = (f32[3,32,24,128]{3,2,1,0:T(8,128)}, f32[3,32,24,128]{3,2,1,0:T(8,128)}, u32[]{:S(2)}, u32[]{:S(2)}) collective-permute-start(f32[3,32,24,128]{3,2,1,0:T(8,128)} %get-tuple-element.71), channel_id=1, source_target_pairs={{0,8},{8,0},{24,16},{1,9},{9,1},{25,17},{2,10},{10,2},{26,18},{3,1... | collective-permute-start | bytes 3538952 | tf_op jit(solution)/shard_map/ppermute | solution.py:292
  29.9 100.3 %collective-permute-start.4 = (f32[3,32,24,128]{3,2,1,0:T(8,128)}, f32[3,32,24,128]{3,2,1,0:T(8,128)}, u32[]{:S(2)}, u32[]{:S(2)}) collective-permute-start(f32[3,32,24,128]{3,2,1,0:T(8,128)} %get-tuple-element.72), channel_id=1, source_target_pairs={{0,16},{16,0},{24,8},{1,17},{17,1},{25,9},{2,18},{18,2},{26,10},{3... | collective-permute-start | bytes 3538952 | tf_op jit(solution)/shard_map/ppermute | solution.py:292
  115.9 29.7 %collective-permute-start.5 = (f32[3,32,24,128]{3,2,1,0:T(8,128)}, f32[3,32,24,128]{3,2,1,0:T(8,128)}, u32[]{:S(2)}, u32[]{:S(2)}) collective-permute-start(f32[3,32,24,128]{3,2,1,0:T(8,128)} %copy-done.22), channel_id=1, source_target_pairs={{8,16},{16,8},{24,0},{9,17},{17,9},{25,1},{10,18},{18,10},{26,2},{... | collective-permute-start | bytes 3538952 | tf_op jit(solution)/shard_map/ppermute | solution.py:292
  123.2 22.4 %copy-start.7 = (f32[3,32,24,128]{3,2,1,0:T(8,128)S(1)}, f32[3,32,24,128]{3,2,1,0:T(8,128)}, u32[]{:S(2)}) copy-start(f32[3,32,24,128]{3,2,1,0:T(8,128)} %copy-done.6) | copy-start | bytes 3538948
  205.8 70.4 %all-to-all-start = ((f32[8,32,2,8,128]{4,3,2,1,0:T(8,128)}), f32[8,32,2,8,128]{4,3,2,1,0:T(8,128)}, u32[]{:S(2)}, u32[]{:S(2)}) async-start(f32[8,32,2,8,128]{4,3,2,1,0:T(8,128)} %get-tuple-element.64), calls=%async_computation | async-start | bytes 4194304 | tf_op jit(solution)/shard_map/all_to_all | solution.py:319
  213.0 29.3 %collective-permute-start.6 = (f32[3,32,24,128]{3,2,1,0:T(8,128)}, f32[3,32,24,128]{3,2,1,0:T(8,128)S(1)}, u32[]{:S(2)}, u32[]{:S(2)}) collective-permute-start(f32[3,32,24,128]{3,2,1,0:T(8,128)} %copy-done.21), channel_id=1, source_target_pairs={{0,8},{8,0},{24,16},{1,9},{9,1},{25,17},{2,10},{10,2},{26,18},{3,1... | collective-permute-start | bytes 3538952 | tf_op jit(solution)/shard_map/ppermute | solution.py:292
  216.1 54.2 %collective-permute-start.7 = (f32[3,32,24,128]{3,2,1,0:T(8,128)}, f32[3,32,24,128]{3,2,1,0:T(8,128)S(1)}, u32[]{:S(2)}, u32[]{:S(2)}) collective-permute-start(f32[3,32,24,128]{3,2,1,0:T(8,128)} %copy-done.20), channel_id=1, source_target_pairs={{0,16},{16,0},{24,8},{1,17},{17,1},{25,9},{2,18},{18,2},{26,10},{3... | collective-permute-start | bytes 3538952 | tf_op jit(solution)/shard_map/ppermute | solution.py:292
  217.4 52.9 %copy-start.5 = (f32[3,32,24,128]{3,2,1,0:T(8,128)S(1)}, f32[3,32,24,128]{3,2,1,0:T(8,128)}, u32[]{:S(2)}) copy-start(f32[3,32,24,128]{3,2,1,0:T(8,128)} %copy-done.4) | copy-start | bytes 3538948
  217.4 52.9 %collective-permute-start.8 = (f32[3,32,24,128]{3,2,1,0:T(8,128)}, f32[3,32,24,128]{3,2,1,0:T(8,128)S(1)}, u32[]{:S(2)}, u32[]{:S(2)}) collective-permute-start(f32[3,32,24,128]{3,2,1,0:T(8,128)} %copy-done.19), channel_id=1, source_target_pairs={{8,16},{16,8},{24,0},{9,17},{17,9},{25,1},{10,18},{18,10},{26,2},{... | collective-permute-start | bytes 3538952 | tf_op jit(solution)/shard_map/ppermute | solution.py:292
  276.2 69.0 %all-to-all-start.2 = ((f32[8,32,2,8,128]{4,3,2,1,0:T(8,128)}), f32[8,32,2,8,128]{4,3,2,1,0:T(8,128)}, u32[]{:S(2)}, u32[]{:S(2)}) async-start(f32[8,32,2,8,128]{4,3,2,1,0:T(8,128)} %get-tuple-element.83), calls=%async_computation.2 | async-start | bytes 4194304 | tf_op jit(solution)/shard_map/all_to_all | solution.py:319
  282.5 54.5 %collective-permute-start.10 = (f32[3,32,24,128]{3,2,1,0:T(8,128)}, f32[3,32,24,128]{3,2,1,0:T(8,128)S(1)}, u32[]{:S(2)}, u32[]{:S(2)}) collective-permute-start(f32[3,32,24,128]{3,2,1,0:T(8,128)} %copy-done.18), channel_id=1, source_target_pairs={{0,16},{16,0},{24,8},{1,17},{17,1},{25,9},{2,18},{18,2},{26,10},{3... | collective-permute-start | bytes 3538952 | tf_op jit(solution)/shard_map/ppermute | solution.py:292
  283.8 53.2 %collective-permute-start.11 = (f32[3,32,24,128]{3,2,1,0:T(8,128)}, f32[3,32,24,128]{3,2,1,0:T(8,128)S(1)}, u32[]{:S(2)}, u32[]{:S(2)}) collective-permute-start(f32[3,32,24,128]{3,2,1,0:T(8,128)} %copy-done.17), channel_id=1, source_target_pairs={{8,16},{16,8},{24,0},{9,17},{17,9},{25,1},{10,18},{18,10},{26,2},{... | collective-permute-start | bytes 3538952 | tf_op jit(solution)/shard_map/ppermute | solution.py:292
  287.8 50.3 %collective-permute-start.9 = (f32[3,32,24,128]{3,2,1,0:T(8,128)}, f32[3,32,24,128]{3,2,1,0:T(8,128)S(1)}, u32[]{:S(2)}, u32[]{:S(2)}) collective-permute-start(f32[3,32,24,128]{3,2,1,0:T(8,128)} %copy-done.16), channel_id=1, source_target_pairs={{0,8},{8,0},{24,16},{1,9},{9,1},{25,17},{2,10},{10,2},{26,18},{3,1... | collective-permute-start | bytes 3538952 | tf_op jit(solution)/shard_map/ppermute | solution.py:292
  345.2 96.4 %all-to-all-start.3 = ((f32[8,32,2,8,128]{4,3,2,1,0:T(8,128)}), f32[8,32,2,8,128]{4,3,2,1,0:T(8,128)}, u32[]{:S(2)}, u32[]{:S(2)}) async-start(f32[8,32,2,8,128]{4,3,2,1,0:T(8,128)} %get-tuple-element.90), calls=%async_computation.3 | async-start | bytes 4194304 | tf_op jit(solution)/shard_map/all_to_all | solution.py:319
  351.5 30.3 %collective-permute-start.12 = (f32[3,32,24,128]{3,2,1,0:T(8,128)}, f32[3,32,24,128]{3,2,1,0:T(8,128)}, u32[]{:S(2)}, u32[]{:S(2)}) collective-permute-start(f32[3,32,24,128]{3,2,1,0:T(8,128)} %copy-done.13), channel_id=1, source_target_pairs={{0,8},{8,0},{24,16},{1,9},{9,1},{25,17},{2,10},{10,2},{26,18},{3,1... | collective-permute-start | bytes 3538952 | tf_op jit(solution)/shard_map/ppermute | solution.py:292
  355.5 79.6 %collective-permute-start.13 = (f32[3,32,24,128]{3,2,1,0:T(8,128)}, f32[3,32,24,128]{3,2,1,0:T(8,128)}, u32[]{:S(2)}, u32[]{:S(2)}) collective-permute-start(f32[3,32,24,128]{3,2,1,0:T(8,128)} %copy-done.12), channel_id=1, source_target_pairs={{0,16},{16,0},{24,8},{1,17},{17,1},{25,9},{2,18},{18,2},{26,10},{3... | collective-permute-start | bytes 3538952 | tf_op jit(solution)/shard_map/ppermute | solution.py:292
  356.8 78.3 %collective-permute-start.14 = (f32[3,32,24,128]{3,2,1,0:T(8,128)S(1)}, f32[3,32,24,128]{3,2,1,0:T(8,128)}, u32[]{:S(2)}, u32[]{:S(2)}) collective-permute-start(f32[3,32,24,128]{3,2,1,0:T(8,128)S(1)} %copy-done.11), channel_id=1, source_target_pairs={{8,16},{16,8},{24,0},{9,17},{17,9},{25,1},{10,18},{18,10},{26,2},{... | collective-permute-start | bytes 3538952 | tf_op jit(solution)/shard_map/ppermute | solution.py:292
  360.5 104.4 %collective-permute-start.15 = (f32[3,32,24,128]{3,2,1,0:T(8,128)}, f32[3,32,24,128]{3,2,1,0:T(8,128)}, u32[]{:S(2)}, u32[]{:S(2)}) collective-permute-start(f32[3,32,24,128]{3,2,1,0:T(8,128)} %copy-done.15), channel_id=1, source_target_pairs={{0,8},{8,0},{24,16},{1,9},{9,1},{25,17},{2,10},{10,2},{26,18},{3,1... | collective-permute-start | bytes 3538952 | tf_op jit(solution)/shard_map/ppermute | solution.py:292
  362.5 102.5 %collective-permute-start.16 = (f32[3,32,24,128]{3,2,1,0:T(8,128)}, f32[3,32,24,128]{3,2,1,0:T(8,128)}, u32[]{:S(2)}, u32[]{:S(2)}) collective-permute-start(f32[3,32,24,128]{3,2,1,0:T(8,128)} %copy-done.14), channel_id=1, source_target_pairs={{0,16},{16,0},{24,8},{1,17},{17,1},{25,9},{2,18},{18,2},{26,10},{3... | collective-permute-start | bytes 3538952 | tf_op jit(solution)/shard_map/ppermute | solution.py:292
  381.8 83.2 %collective-permute-start.17 = (f32[3,32,24,128]{3,2,1,0:T(8,128)}, f32[3,32,24,128]{3,2,1,0:T(8,128)}, u32[]{:S(2)}, u32[]{:S(2)}) collective-permute-start(f32[3,32,24,128]{3,2,1,0:T(8,128)} %get-tuple-element.103), channel_id=1, source_target_pairs={{8,16},{16,8},{24,0},{9,17},{17,9},{25,1},{10,18},{18,10},{26,2},{... | collective-permute-start | bytes 3538952 | tf_op jit(solution)/shard_map/ppermute | solution.py:292
  441.6 52.9 %all-to-all-start.4 = ((f32[8,32,2,8,128]{4,3,2,1,0:T(8,128)}), f32[8,32,2,8,128]{4,3,2,1,0:T(8,128)}, u32[]{:S(2)}, u32[]{:S(2)}) async-start(f32[8,32,2,8,128]{4,3,2,1,0:T(8,128)} %get-tuple-element.97), calls=%async_computation.4 | async-start | bytes 4194304 | tf_op jit(solution)/shard_map/all_to_all | solution.py:319
  494.5 74.6 %all-to-all-start.5 = ((f32[8,40,2,8,128]{4,3,2,1,0:T(8,128)}), f32[8,40,2,8,128]{4,3,2,1,0:T(8,128)}, u32[]{:S(2)}, u32[]{:S(2)}) async-start(f32[8,40,2,8,128]{4,3,2,1,0:T(8,128)} %get-tuple-element.104), calls=%async_computation.5 | async-start | bytes 5242880 | tf_op jit(solution)/shard_map/all_to_all | solution.py:319
  620.4 30.6 %copy-start.27 = (f32[2,8,32,1536]{3,2,1,0:T(8,128)S(1)}, f32[2,8,32,1536]{3,2,1,0:T(8,128)}, u32[]{:S(2)}) copy-start(f32[2,8,32,1536]{3,2,1,0:T(8,128)} %get-tuple-element.152) | copy-start | bytes 9437188
  620.4 30.6 %copy-start.28 = (f32[2,8,32,1536]{3,2,1,0:T(8,128)S(1)}, f32[2,8,32,1536]{3,2,1,0:T(8,128)}, u32[]{:S(2)}) copy-start(f32[2,8,32,1536]{3,2,1,0:T(8,128)} %get-tuple-element.153) | copy-start | bytes 9437188
  (29 other events, 120.0 us)
